TPU v7x, 32 devices: a whole 2x2x4 slice. The times are simulated.
32 devices in a mesh: dom: 8 (over z, x), slab: 4 (over y, core).
Axes of the slice: x: 2, y: 2, z: 4, core: 2. Of those that a mesh axis runs over, the one named last changes fastest.
Arguments:
- basis_weights: float32 [4, 4, 12288], P(None, 'slab', 'dom'), may hold values from 0 to 1, as said below
- velocity: float32 [3, 4, 12288], P(None, 'slab', 'dom'), may hold values from -6 to 6
- owner_dom: int32 [4, 12288, 1], P('slab', 'dom'), may hold values from 0 to 7; in each aligned block of 1536 rows (0 to 1535, 1536 to 3071, ..., all dimensions but the last counted through in order) at most 384 rows name the same one
- cell_local: int32 [4, 12288], P('slab', 'dom'), may hold values from 0 to 255
- inverse: float32 [16, 4, 2048], P(None, 'slab', 'dom'), may hold values from -0.2 to 1.5
- connectivity: int32 [4, 4, 2048], P(None, 'slab', 'dom'), may hold values from 0 to 2303, as said below
Outputs:
- coefficients: float32 [12, 4, 2048], P(None, 'slab', 'dom')
- node_values: float32 [3, 4, 2048], P(None, 'slab', 'dom')
Inputs may be any that keep to these rules, and one draw needn't show every extreme that they name: `basis_weights`: the four entries of each particle are positive and sum to one. `owner_dom`: among the rows of one device, no owner is named more than 384 times. `connectivity`: the slab move and dom move are each -1, 0 or 1, and the node they name lies inside the domain.
All inputs are finite; a program needn't handle non-finite values.
Results may differ from a plain program's by a relative error of at most 0.00011.
Values sent between devices are 32-bit elements; how exact they have to be, the bound alone decides.
No kernel may reach another device: no remote copies, remote signals or barrier semaphores. Data moves between devices by JAX's collectives and lax.ppermute only.
A program may use at most 64 MiB of HBM per device.

v0:
```python
import math
import jax
import jax.numpy as jnp
import numpy as np
from jax import lax
from jax.sharding import PartitionSpec as P

NODES_DEV = 256
PAIR_FIRST = np.array([0, 0, 0, 0, 1, 1, 1, 2, 2, 3], dtype=np.int32)
PAIR_SECOND = np.array([0, 1, 2, 3, 1, 2, 3, 2, 3, 3], dtype=np.int32)
GRAM_FROM_PAIR = np.array([0, 1, 2, 3, 1, 4, 5, 6, 2, 5, 7, 8, 3, 6, 8, 9], dtype=np.int32)


def from_behind(array, axis, by):
    devices = lax.axis_size(axis)
    pairs = [(i, i + by) for i in range(devices) if 0 <= i + by < devices]
    return lax.ppermute(array, axis, pairs)


def expand_terms(weights, velocities):
    upper_terms = weights[PAIR_FIRST] * weights[PAIR_SECOND]
    moment_terms = (weights[:, None, :] * velocities[None, :, :]).reshape(12, -1)
    return jnp.concatenate([upper_terms, moment_terms], axis=0)


def onehot_sum(values, segment_ids, segment_count):
    total = segment_ids.shape[0]
    row_count = values.shape[0]
    limit = max(128, 2097152 // segment_count)
    block = math.gcd(total, limit)
    rounds = total // block
    value_blocks = jnp.transpose(values.reshape(row_count, rounds, block), (1, 0, 2))
    id_blocks = segment_ids.reshape(rounds, block)
    columns = jnp.arange(segment_count, dtype=jnp.int32)

    def accumulate(carry, items):
        value_block, id_block = items
        table = (id_block[:, None] == columns[None, :]).astype(jnp.float32)
        return (
            carry
            + jnp.dot(
                value_block,
                table,
                precision=lax.Precision.HIGHEST,
                preferred_element_type=jnp.float32,
            ),
            None,
        )

    start = jnp.zeros((row_count, segment_count), jnp.float32)
    result, unused = lax.scan(accumulate, start, (value_blocks, id_blocks))
    return result


def per_device(basis_weights, velocity, owner_dom, cell_local, inverse, connectivity):
    particles = basis_weights.shape[2]
    cell_count = inverse.shape[2]
    dom_count = lax.axis_size("dom")
    capacity = 2 * particles // dom_count
    slot_count = dom_count * capacity
    destination = owner_dom.reshape(particles)
    sort_order = jnp.argsort(destination, stable=True)
    ranked = destination[sort_order]
    starts = jnp.searchsorted(ranked, jnp.arange(dom_count, dtype=jnp.int32))
    slot_index = ranked * capacity + jnp.arange(particles, dtype=jnp.int32) - starts[ranked]
    weights = basis_weights[:, 0]
    velocities = velocity[:, 0]
    cell_float = cell_local.astype(jnp.float32)
    payload = jnp.concatenate([weights, velocities, cell_float], axis=0)
    empty = jnp.zeros((payload.shape[0], slot_count), jnp.float32)
    outgoing = empty.at[:, slot_index].set(payload[:, sort_order])
    arrived = lax.all_to_all(outgoing, "dom", split_axis=1, concat_axis=1, tiled=True)
    products = expand_terms(arrived[:4], arrived[4:7])
    cell_index = arrived[7].astype(jnp.int32)
    totals = onehot_sum(products, cell_index, cell_count)
    gram_full = totals[:10][GRAM_FROM_PAIR].reshape(4, 4, cell_count)
    moment = totals[10:].reshape(4, 3, cell_count)
    matrix = inverse[:, 0].reshape(4, 4, cell_count)
    first_pass = jnp.sum(matrix[:, :, None, :] * moment[None], axis=1)
    residual_part = moment - jnp.sum(gram_full[:, :, None, :] * first_pass[None], axis=1)
    solved = first_pass + jnp.sum(matrix[:, :, None, :] * residual_part[None], axis=1)
    coefficients = solved.reshape(12, 1, cell_count)
    node_count = NODES_DEV
    bucket = connectivity[:, 0]
    corner_values = jnp.transpose(solved, (1, 0, 2)).reshape(3, 4 * cell_count)
    local_sums = onehot_sum(corner_values, bucket.reshape(-1), 9 * node_count).reshape(
        3, 3, 3, node_count
    )
    from_below = from_behind(local_sums[:, :, 2], "dom", 1)
    from_above = from_behind(local_sums[:, :, 0], "dom", -1)
    merged = local_sums[:, :, 1] + from_below + from_above
    slab_below = from_behind(merged[:, 2], "slab", 1)
    slab_above = from_behind(merged[:, 0], "slab", -1)
    node_values = (merged[:, 1] + slab_below + slab_above).reshape(3, 1, node_count)
    return (coefficients, node_values)


def solution(mesh):
    in_specs = (
        P(None, "slab", "dom"),
        P(None, "slab", "dom"),
        P("slab", "dom", None),
        P("slab", "dom"),
        P(None, "slab", "dom"),
        P(None, "slab", "dom"),
    )
    out_specs = (P(None, "slab", "dom"), P(None, "slab", "dom"))
    return jax.shard_map(
        per_device, mesh=mesh, in_specs=in_specs, out_specs=out_specs, check_vma=False
    )
```

profile of v0, /device:TPU:1, one launch (start us, length us, event | category | flops | bytes accessed | tf_op | source)
XLA Modules:
  0.0 230.3 jit_solution(17716945003019900651)
XLA Ops:
  0.6 0.7 reduce
  1.4 5.0 %sort.17 = (s32[1536]{0:T(1024)}, s32[1536]{0:T(1024)S(1)}) sort(s32[1536]{0:T(1024)S(1)} %reduce, s32[1536]{0:T(1024)S(1)} %iota.17), dimensions={0}, to_apply=%region_0.0 | sort | flops 16896 | bytes 24576 | tf_op jit(solution)/shard_map/jit(argsort)/sort | solution.py:62
  6.4 8.4 %gather_fusion.1 = s32[1536]{0:T(1024)S(1)} fusion(s32[1536]{0:T(1024)S(1)} %reduce, s32[2048]{0:T(1024)S(1)} %pad_clamp_fusion.1), kind=kCustom, calls=%fused_computation.1 | custom fusion | bytes 18432 | tf_op jit(solution)/shard_map/gather | solution.py:63
  14.9 7.6 %while.46 = (s32[]{:T(128)}, u32[8]{0:T(128)S(1)}, u32[8]{0:T(128)S(1)}, s32[1536]{0:T(1024)S(1)}, s32[]{:T(128)}, /*index=5*/s32[]{:T(128)}, s32[]{}) while((s32[]{:T(128)}, u32[8]{0:T(128)S(1)}, u32[8]{0:T(128)S(1)}, s32[1536]{0:T(1024)S(1)}, s32[]{:T(128)}, /*index=5*/s32[]{:T(128)}, s32[]{}) %tuple.91), condition=%wide.region_2.3_spmd.clone, body=%wide.region_1.2_spmd.clone.sunk | while | flops 1132 | bytes 4580 | solution.py:64
  14.9 0.6 gather_fusion
  15.6 0.6 gather_fusion
  16.3 0.6 gather_fusion
  17.0 0.6 gather_fusion
  17.7 0.6 gather_fusion
  18.4 0.6 gather_fusion
  19.1 0.6 gather_fusion
  19.8 0.6 gather_fusion
  20.5 0.6 gather_fusion
  21.2 0.6 gather_fusion
  21.9 0.6 gather_fusion
  22.5 0.7 fusion.28
  23.2 4.4 %fusion.21 = s32[1536]{0:T(1024)S(1)} fusion(s32[]{:T(128)} %bitcast.1, s32[]{:T(128)} %bitcast.2, s32[]{:T(128)} %bitcast.3, s32[]{:T(128)} %bitcast.4, s32[]{:T(128)} %bitcast.5, s32[]{:T(128)} %bitcast.7, s32[]{:T(128)} %bitcast.6, s32[1536]{0:T(1024)S(1)} %get-tuple-element.381), kind=kLoop, calls=%fused_computation.60 | loop fusion | flops 23040 | bytes 12316 | tf_op jit(solution)/shard_map/gather | solution.py:65
  27.7 0.7 broadcast_select_fusion.2
  28.8 10.0 %scatter_custom_fusion = f32[8,3072]{0,1:T(8,128)S(1)} fusion(s32[1536]{0:T(1024)S(1)} %fusion.22, f32[8,1536]{0,1:T(8,128)S(1)} %copy.55, s32[2048]{0:T(1024)S(1)} %pad_clamp_fusion.1, f32[]{:T(128)} %constant.69.clone.1), kind=kCustom, calls=%fused_computation.31 | custom fusion | bytes 98308 | tf_op jit(solution)/shard_map/scatter | solution.py:71
  38.8 1.1 copy.56
  39.9 6.4 %all-to-all-start = ((f32[8,8,384]{2,0,1:T(8,128)}), f32[8,8,384]{2,0,1:T(8,128)S(1)}, u32[]{:S(2)}, u32[]{:S(2)}) async-start(f32[8,8,384]{2,0,1:T(8,128)} %copy.56), calls=%async_computation | async-start | bytes 196608 | tf_op jit(solution)/shard_map/all_to_all | solution.py:72
  46.6 5.7 %all-to-all-done = f32[8,8,384]{2,0,1:T(8,128)S(1)} async-done(((f32[8,8,384]{2,0,1:T(8,128)}), f32[8,8,384]{2,0,1:T(8,128)S(1)}, u32[]{:S(2)}, u32[]{:S(2)}) %all-to-all-start) | async-done | bytes 98336 | tf_op jit(solution)/shard_map/all_to_all | solution.py:72
  52.3 0.6 gather_fusion.2
  52.9 0.6 gather_fusion.3
  54.0 2.0 while.47
  54.2 0.5 convolution_add_fusion.4
  54.8 0.5 convolution_add_fusion.4
  55.5 0.5 convolution_add_fusion.4
  56.1 0.6 gather_fusion.4
  56.9 0.8 reshape_reshape.3
  57.6 3.2 %copy.62 = f32[512,3,2]{1,2,0:T(2,128)S(1)} copy(f32[512,3,2]{2,0,1:T(8,128)S(1)} %bitcast.70) | data formatting | bytes 24576
  60.9 150.9 %while.48 = (s32[]{:T(128)}, f32[3,2304]{1,0:T(4,128)S(1)}, f32[512,3,2]{1,2,0:T(2,128)S(1)}, s32[512,2]{1,0:T(8,128)S(1)}, s32[]{:T(128)}, /*index=5*/s32[]{:T(128)}) while((s32[]{:T(128)}, f32[3,2304]{1,0:T(4,128)S(1)}, f32[512,3,2]{1,2,0:T(2,128)S(1)}, s32[512,2]{1,0:T(8,128)S(1)}, s32[]{:T(128)}, /*index=5*/s32[]{:T(128)}) %tuple.97), condition=%wide.region_10.11_spmd.clone, body=%wide.region_9.10_spmd.clone.sunk | while | flops 184323 | bytes 66151 | solution.py:51
  60.9 0.3 convolution_add_fusion.5
  62.1 0.3 convolution_add_fusion.5
  62.4 0.3 convolution_add_fusion.5
  62.7 0.3 convolution_add_fusion.5
  63.0 0.3 convolution_add_fusion.5
  63.8 0.3 convolution_add_fusion.5
  64.1 0.3 convolution_add_fusion.5
  64.4 0.3 convolution_add_fusion.5
  64.7 0.3 convolution_add_fusion.5
  65.9 0.3 convolution_add_fusion.5
  66.2 0.3 convolution_add_fusion.5
  66.5 0.3 convolution_add_fusion.5
  67.7 0.3 convolution_add_fusion.5
  68.0 0.3 convolution_add_fusion.5
  68.3 0.3 convolution_add_fusion.5
  68.6 0.3 convolution_add_fusion.5
  69.4 0.3 convolution_add_fusion.5
  69.7 0.3 convolution_add_fusion.5
  70.0 0.3 convolution_add_fusion.5
  70.3 0.3 convolution_add_fusion.5
  71.5 0.3 convolution_add_fusion.5
  71.8 0.3 convolution_add_fusion.5
  72.1 0.3 convolution_add_fusion.5
  73.3 0.3 convolution_add_fusion.5
  211.8 1.8 collective-permute-start
  213.7 1.3 collective-permute-start.1
  215.0 3.1 %collective-permute-done.1 = f32[3,3,256]{2,1,0:T(4,128)S(1)} collective-permute-done((f32[3,3,256]{2,1,0:T(4,128)S(1)}, f32[3,3,256]{2,1,0:T(4,128)S(1)}, u32[]{:S(2)}, u32[]{:S(2)}) %collective-permute-start.1) | collective-permute-done | bytes 9248 | tf_op jit(solution)/shard_map/ppermute | solution.py:17
  218.2 6.6 %collective-permute-start.2 = (f32[3,256]{1,0:T(4,128)S(1)}, f32[3,256]{1,0:T(4,128)S(1)}, u32[]{:S(2)}, u32[]{:S(2)}) collective-permute-start(f32[3,256]{1,0:T(4,128)S(1)} %bitcast.78), channel_id=1, source_target_pairs={{0,1},{1,2},{2,3},{4,5},{5,6},{6,7},{8,9},{9,10},{10,11},{12,13},{... | collective-permute-start | bytes 9224 | tf_op jit(solution)/shard_map/ppermute | solution.py:17
  224.8 1.9 collective-permute-start.3
  226.7 0.6 add.127
  227.3 2.4 %collective-permute-done.3 = f32[3,256]{1,0:T(4,128)S(1)} collective-permute-done((f32[3,256]{1,0:T(4,128)S(1)}, f32[3,256]{1,0:T(4,128)S(1)}, u32[]{:S(2)}, u32[]{:S(2)}) %collective-permute-start.3) | collective-permute-done | bytes 3104 | tf_op jit(solution)/shard_map/ppermute | solution.py:17
  229.7 0.6 copy.68
  (1110 shorter events, 135.1 us)
Async XLA Ops:
  14.8 13.5 %copy-start.1 = (f32[3,1,1536]{2,1,0:T(1,128)S(1)}, f32[3,1,1536]{2,1,0:T(1,128)}, u32[]{:S(2)}) copy-start(f32[3,1,1536]{2,1,0:T(1,128)} %param.19) | copy-start | bytes 55300
  14.8 13.6 %copy-start = (f32[4,1,1536]{2,1,0:T(1,128)S(1)}, f32[4,1,1536]{2,1,0:T(1,128)}, u32[]{:S(2)}) copy-start(f32[4,1,1536]{2,1,0:T(1,128)} %param.18) | copy-start | bytes 73732
  14.8 13.6 %copy-start.3 = (s32[1,1536]{1,0:T(1,128)S(1)}, s32[1,1536]{1,0:T(1,128)}, u32[]{:S(2)}) copy-start(s32[1,1536]{1,0:T(1,128)} %param.21) | copy-start | bytes 18436
  28.7 17.5 %copy-start.7 = (s32[10]{0:T(128)S(1)}, s32[10]{0:T(128)}, u32[]{:S(2)}) copy-start(s32[10]{0:T(128)} %constant.99) | copy-start | bytes 124
  28.8 17.5 %copy-start.2 = (f32[16,1,256]{2,1,0:T(1,128)S(1)}, f32[16,1,256]{2,1,0:T(1,128)}, u32[]{:S(2)}) copy-start(f32[16,1,256]{2,1,0:T(1,128)} %param.22) | copy-start | bytes 49156
  28.8 17.6 %copy-start.4 = (s32[4,1,256]{2,1,0:T(1,128)S(1)}, s32[4,1,256]{2,1,0:T(1,128)}, u32[]{:S(2)}) copy-start(s32[4,1,256]{2,1,0:T(1,128)} %param.23) | copy-start | bytes 12292
  28.8 17.8 %copy-start.6 = (s32[10]{0:T(128)S(1)}, s32[10]{0:T(128)}, u32[]{:S(2)}) copy-start(s32[10]{0:T(128)} %constant.100) | copy-start | bytes 124
  28.8 17.8 %copy-start.5 = (s32[16]{0:T(128)S(1)}, s32[16]{0:T(128)}, u32[]{:S(2)}) copy-start(s32[16]{0:T(128)} %constant.101) | copy-start | bytes 196
  39.9 12.4 %all-to-all-start = ((f32[8,8,384]{2,0,1:T(8,128)}), f32[8,8,384]{2,0,1:T(8,128)S(1)}, u32[]{:S(2)}, u32[]{:S(2)}) async-start(f32[8,8,384]{2,0,1:T(8,128)} %copy.56), calls=%async_computation | async-start | bytes 196608 | tf_op jit(solution)/shard_map/all_to_all | solution.py:72
  211.8 3.1 %collective-permute-start = (f32[3,3,256]{2,1,0:T(4,128)S(1)}, f32[3,3,256]{2,1,0:T(4,128)S(1)}, u32[]{:S(2)}, u32[]{:S(2)}) collective-permute-start(f32[3,3,256]{2,1,0:T(4,128)S(1)} %bitcast.76), channel_id=1, source_target_pairs={{0,4},{4,8},{8,12},{12,16},{16,20},{20,24},{24,28},{1,5},{5,9},{9,... | collective-permute-start | bytes 27656 | tf_op jit(solution)/shard_map/ppermute | solution.py:17
  213.7 4.4 %collective-permute-start.1 = (f32[3,3,256]{2,1,0:T(4,128)S(1)}, f32[3,3,256]{2,1,0:T(4,128)S(1)}, u32[]{:S(2)}, u32[]{:S(2)}) collective-permute-start(f32[3,3,256]{2,1,0:T(4,128)S(1)} %bitcast.77), channel_id=1, source_target_pairs={{4,0},{8,4},{12,8},{16,12},{20,16},{24,20},{28,24},{5,1},{9,5},{13... | collective-permute-start | bytes 27656 | tf_op jit(solution)/shard_map/ppermute | solution.py:17
  218.2 9.1 %collective-permute-start.2 = (f32[3,256]{1,0:T(4,128)S(1)}, f32[3,256]{1,0:T(4,128)S(1)}, u32[]{:S(2)}, u32[]{:S(2)}) collective-permute-start(f32[3,256]{1,0:T(4,128)S(1)} %bitcast.78), channel_id=1, source_target_pairs={{0,1},{1,2},{2,3},{4,5},{5,6},{6,7},{8,9},{9,10},{10,11},{12,13},{... | collective-permute-start | bytes 9224 | tf_op jit(solution)/shard_map/ppermute | solution.py:17
  224.8 4.9 %collective-permute-start.3 = (f32[3,256]{1,0:T(4,128)S(1)}, f32[3,256]{1,0:T(4,128)S(1)}, u32[]{:S(2)}, u32[]{:S(2)}) collective-permute-start(f32[3,256]{1,0:T(4,128)S(1)} %bitcast.79), channel_id=1, source_target_pairs={{1,0},{2,1},{3,2},{5,4},{6,5},{7,6},{9,8},{10,9},{11,10},{13,12},{... | collective-permute-start | bytes 9224 | tf_op jit(solution)/shard_map/ppermute | solution.py:17
where the time goes:
time: 231 us; the launch traced here: 230 us
  matrix products  136 us (59%)
  local copies, waits for them, and re-layouts  40.2 us (17%)
  starting transfers between devices  18 us (8%)
  loops' own time  12 us (5%)
  other arithmetic  11.7 us (5%)
  waiting for transfers between devices  11.2 us (5%)
    dot_general x515, matrix products, accumulate(): jnp.dot(value_block, table, precision=lax.Precision.HIGHEST, preferred_el...  136 us
    another operation x2, loops' own time, onehot_sum(): result, unused = lax.scan(accumulate, start, (value_blocks, id_blocks))  11.7 us
    ppermute x4, starting transfers between devices, from_behind(): return lax.ppermute(array, axis, pairs)  11.6 us
    scatter x1, local copies, waits for them, and re-layouts, per_device(): outgoing = empty.at[:, slot_index].set(payload[:, sort_order])  10 us
    gather x1, local copies, waits for them, and re-layouts, per_device(): ranked = destination[sort_order]  8.39 us
    gather x11, local copies, waits for them, and re-layouts, per_device(): starts = jnp.searchsorted(ranked, jnp.arange(dom_count, dtype=jnp.int32))  6.99 us
    all_to_all x1, starting transfers between devices, per_device(): lax.all_to_all(outgoing, 'dom', split_axis=1, concat_axis=1, tiled=True)  6.35 us
    all_to_all x1, waiting for transfers between devices, per_device(): lax.all_to_all(outgoing, 'dom', split_axis=1, concat_axis=1, tiled=True)  5.68 us
  transfers between devices with their start and end apart: 5, of which 3 were waited for; matrix products, arithmetic and copies ran while one was open for 0% of the time, Pallas kernels for 0%

commit v1 on v0

--- a/solution.py
+++ b/solution.py
@@ -9,6 +9,21 @@
 PAIR_FIRST = np.array([0, 0, 0, 0, 1, 1, 1, 2, 2, 3], dtype=np.int32)
 PAIR_SECOND = np.array([0, 1, 2, 3, 1, 2, 3, 2, 3, 3], dtype=np.int32)
 GRAM_FROM_PAIR = np.array([0, 1, 2, 3, 1, 4, 5, 6, 2, 5, 7, 8, 3, 6, 8, 9], dtype=np.int32)
+
+
+def answer_domain(content, d0, here_x):
+    odd = content.shape
+    local_now = jnp.moveaxis(
+        content.reshape(*odd[:d0], here_x, odd[d0] // here_x, *odd[d0 + 1 :]), d0, 0
+    )
+    return local_now
+
+
+def place_sheet(xx, dim_no):
+    frame_out = list(xx.shape[1:])
+    frame_out[dim_no] *= xx.shape[0]
+    local_part = jnp.moveaxis(xx, 0, dim_no).reshape(frame_out)
+    return local_part
 
 
 def from_behind(array, axis, by):
@@ -69,7 +84,19 @@
     payload = jnp.concatenate([weights, velocities, cell_float], axis=0)
     empty = jnp.zeros((payload.shape[0], slot_count), jnp.float32)
     outgoing = empty.at[:, slot_index].set(payload[:, sort_order])
-    arrived = lax.all_to_all(outgoing, "dom", split_axis=1, concat_axis=1, tiled=True)
+    carry_out, y2 = (lax.psum(1, axis_name="dom"), lax.axis_index("dom"))
+    y_new = answer_domain(outgoing, 1, carry_out)
+    n_now = y_new
+    for to_i in range(1, carry_out):
+        later, t1 = ((y2 + to_i) % carry_out, (y2 - to_i) % carry_out)
+        aux = lax.dynamic_index_in_dim(y_new, later, 0)
+        value_now = lax.ppermute(
+            aux,
+            axis_name="dom",
+            perm=[(hop_no, (hop_no + to_i) % carry_out) for hop_no in range(carry_out)],
+        )
+        n_now = lax.dynamic_update_slice_in_dim(n_now, value_now, t1, axis=0)
+    arrived = place_sheet(n_now, 1)
     products = expand_terms(arrived[:4], arrived[4:7])
     cell_index = arrived[7].astype(jnp.int32)
     totals = onehot_sum(products, cell_index, cell_count)

time: 231 us -> 231 us (level)
  waiting for transfers between devices: 11.2 us -> 3.26 us
  starting transfers between devices: 18 us -> 25.6 us
    ppermute x0 -> x7, starting transfers between devices: none -> 11.4 us  [per_device(): lax.ppermute(aux, axis_name='dom', perm=[(hop_no, (hop_no + to_i) % carry...]
    all_to_all x1 -> x0, starting transfers between devices: 6.35 us -> none  [per_device(): lax.all_to_all(outgoing, 'dom', split_axis=1, concat_axis=1, tiled=True)]
    all_to_all x1 -> x0, waiting for transfers between devices: 5.68 us -> none  [per_device(): lax.all_to_all(outgoing, 'dom', split_axis=1, concat_axis=1, tiled=True)]
    ppermute x4, starting transfers between devices: 11.6 us -> 14.2 us  [from_behind(): return lax.ppermute(array, axis, pairs)]
  transfers between devices with their start and end apart: 5 -> 11, of which waited for: 3 -> 2; matrix products, arithmetic and copies ran while one was open for 0% -> 1% of each run, Pallas kernels for 0% -> 0%
where the time goes in v1:
time: 231 us
  matrix products  136 us (59%)
  local copies, waits for them, and re-layouts  40.8 us (18%)
  starting transfers between devices  25.6 us (11%)
  loops' own time  12 us (5%)
  other arithmetic  11.6 us (5%)
  waiting for transfers between devices  3.26 us (1%)
    dot_general x515, matrix products, accumulate(): jnp.dot(value_block, table, precision=lax.Precision.HIGHEST, preferred_el...  136 us
    ppermute x4, starting transfers between devices, from_behind(): return lax.ppermute(array, axis, pairs)  14.2 us
    another operation x2, loops' own time, onehot_sum(): result, unused = lax.scan(accumulate, start, (value_blocks, id_blocks))  11.7 us
    ppermute x7, starting transfers between devices, per_device(): lax.ppermute(aux, axis_name='dom', perm=[(hop_no, (hop_no + to_i) % carry...  11.4 us
    scatter x1, local copies, waits for them, and re-layouts, per_device(): outgoing = empty.at[:, slot_index].set(payload[:, sort_order])  10 us
    gather x1, local copies, waits for them, and re-layouts, per_device(): ranked = destination[sort_order]  8.39 us
    gather x11, local copies, waits for them, and re-layouts, per_device(): starts = jnp.searchsorted(ranked, jnp.arange(dom_count, dtype=jnp.int32))  6.99 us
    gather x3, other arithmetic, per_device(): starts[ranked]  5.11 us
  transfers between devices with their start and end apart: 11, of which 2 were waited for; matrix products, arithmetic and copies ran while one was open for 1% of the time, Pallas kernels for 0%

profile of v1, /device:TPU:1, one launch (start us, length us, event | category | flops | bytes accessed | tf_op | source)
XLA Modules:
  0.0 231.0 jit_solution(15510239181098485924)
XLA Ops:
  0.7 0.7 reduce
  1.5 5.0 %sort.17 = (s32[1536]{0:T(1024)}, s32[1536]{0:T(1024)S(1)}) sort(s32[1536]{0:T(1024)S(1)} %reduce, s32[1536]{0:T(1024)S(1)} %iota.17), dimensions={0}, to_apply=%region_0.0 | sort | flops 16896 | bytes 24576 | tf_op jit(solution)/shard_map/jit(argsort)/sort | solution.py:77
  6.5 8.4 %gather_fusion.1 = s32[1536]{0:T(1024)S(1)} fusion(s32[1536]{0:T(1024)S(1)} %reduce, s32[2048]{0:T(1024)S(1)} %pad_clamp_fusion.1), kind=kCustom, calls=%fused_computation.1 | custom fusion | bytes 18432 | tf_op jit(solution)/shard_map/gather | solution.py:78
  15.0 7.6 %while.46 = (s32[]{:T(128)}, u32[8]{0:T(128)S(1)}, u32[8]{0:T(128)S(1)}, s32[1536]{0:T(1024)S(1)}, s32[]{:T(128)}, /*index=5*/s32[]{:T(128)}, s32[]{}) while((s32[]{:T(128)}, u32[8]{0:T(128)S(1)}, u32[8]{0:T(128)S(1)}, s32[1536]{0:T(1024)S(1)}, s32[]{:T(128)}, /*index=5*/s32[]{:T(128)}, s32[]{}) %tuple.97), condition=%wide.region_2.3_spmd.clone, body=%wide.region_1.2_spmd.clone.sunk | while | flops 1132 | bytes 4580 | solution.py:79
  15.0 0.6 gather_fusion
  15.7 0.6 gather_fusion
  16.4 0.6 gather_fusion
  17.1 0.6 gather_fusion
  17.8 0.6 gather_fusion
  18.5 0.6 gather_fusion
  19.2 0.6 gather_fusion
  19.9 0.6 gather_fusion
  20.6 0.6 gather_fusion
  21.3 0.6 gather_fusion
  22.0 0.6 gather_fusion
  22.6 0.7 fusion.27
  23.3 4.4 %fusion.20 = s32[1536]{0:T(1024)S(1)} fusion(s32[]{:T(128)} %bitcast.1, s32[]{:T(128)} %bitcast.2, s32[]{:T(128)} %bitcast.3, s32[]{:T(128)} %bitcast.4, s32[]{:T(128)} %bitcast.5, s32[]{:T(128)} %bitcast.7, s32[]{:T(128)} %bitcast.6, s32[1536]{0:T(1024)S(1)} %get-tuple-element.388), kind=kLoop, calls=%fused_computation.61 | loop fusion | flops 23040 | bytes 12316 | tf_op jit(solution)/shard_map/gather | solution.py:80
  27.8 0.7 broadcast_select_fusion.2
  28.9 10.0 %scatter_custom_fusion = f32[8,3072]{0,1:T(8,128)S(1)} fusion(s32[1536]{0:T(1024)S(1)} %fusion.21, f32[8,1536]{0,1:T(8,128)S(1)} %copy.76, s32[2048]{0:T(1024)S(1)} %pad_clamp_fusion.1, f32[]{:T(128)} %constant.165.clone.1), kind=kCustom, calls=%fused_computation.31 | custom fusion | bytes 98308 | tf_op jit(solution)/shard_map/scatter | solution.py:86
  39.1 2.1 collective-permute-start
  41.3 1.3 collective-permute-start.1
  42.7 2.3 %collective-permute-start.2 = (f32[1,8,384]{2,0,1:T(1,128)S(1)}, f32[1,8,384]{2,0,1:T(1,128)S(1)}, u32[]{:S(2)}, u32[]{:S(2)}) collective-permute-start(f32[1,8,384]{2,0,1:T(1,128)S(1)} %bitcast.98), channel_id=1, source_target_pairs={{0,12},{4,16},{8,20},{12,24},{16,28},{20,0},{24,4},{28,8},{1,13},{... | collective-permute-start | bytes 36872 | tf_op jit(solution)/shard_map/ppermute | solution.py:93
  45.1 1.0 collective-permute-start.3
  46.2 2.4 %collective-permute-start.4 = (f32[1,8,384]{2,0,1:T(1,128)S(1)}, f32[1,8,384]{2,0,1:T(1,128)S(1)}, u32[]{:S(2)}, u32[]{:S(2)}) collective-permute-start(f32[1,8,384]{2,0,1:T(1,128)S(1)} %bitcast.95), channel_id=1, source_target_pairs={{0,20},{4,24},{8,28},{12,0},{16,4},{20,8},{24,12},{28,16},{1,21},{... | collective-permute-start | bytes 36872 | tf_op jit(solution)/shard_map/ppermute | solution.py:93
  48.8 1.1 collective-permute-start.5
  49.9 1.2 collective-permute-start.6
  51.1 0.4 copy.77
  52.7 0.6 gather_fusion.2
  53.3 0.6 gather_fusion.3
  54.4 2.0 while.47
  54.5 0.5 convolution_add_fusion.4
  55.2 0.5 convolution_add_fusion.4
  55.9 0.5 convolution_add_fusion.4
  56.5 0.6 gather_fusion.4
  57.2 0.8 reshape_reshape.3
  58.0 3.2 %copy.90 = f32[512,3,2]{1,2,0:T(2,128)S(1)} copy(f32[512,3,2]{2,0,1:T(8,128)S(1)} %bitcast.84) | data formatting | bytes 24576
  61.2 150.9 %while.48 = (s32[]{:T(128)}, f32[3,2304]{1,0:T(4,128)S(1)}, f32[512,3,2]{1,2,0:T(2,128)S(1)}, s32[512,2]{1,0:T(8,128)S(1)}, s32[]{:T(128)}, /*index=5*/s32[]{:T(128)}) while((s32[]{:T(128)}, f32[3,2304]{1,0:T(4,128)S(1)}, f32[512,3,2]{1,2,0:T(2,128)S(1)}, s32[512,2]{1,0:T(8,128)S(1)}, s32[]{:T(128)}, /*index=5*/s32[]{:T(128)}) %tuple.103), condition=%wide.region_10.11_spmd.clone, body=%wide.region_9.10_spmd.clone.sunk | while | flops 184323 | bytes 66151 | solution.py:66
  61.2 0.3 convolution_add_fusion.5
  61.5 0.3 convolution_add_fusion.5
  61.8 0.3 convolution_add_fusion.5
  62.1 0.3 convolution_add_fusion.5
  63.3 0.3 convolution_add_fusion.5
  63.6 0.3 convolution_add_fusion.5
  63.9 0.3 convolution_add_fusion.5
  65.1 0.3 convolution_add_fusion.5
  65.4 0.3 convolution_add_fusion.5
  65.7 0.3 convolution_add_fusion.5
  66.0 0.3 convolution_add_fusion.5
  66.9 0.3 convolution_add_fusion.5
  67.1 0.3 convolution_add_fusion.5
  67.4 0.3 convolution_add_fusion.5
  67.7 0.3 convolution_add_fusion.5
  68.9 0.3 convolution_add_fusion.5
  69.2 0.3 convolution_add_fusion.5
  69.5 0.3 convolution_add_fusion.5
  70.7 0.3 convolution_add_fusion.5
  71.0 0.3 convolution_add_fusion.5
  212.2 3.0 %collective-permute-start.7 = (f32[3,3,256]{2,1,0:T(4,128)S(1)}, f32[3,3,256]{2,1,0:T(4,128)S(1)}, u32[]{:S(2)}, u32[]{:S(2)}) collective-permute-start(f32[3,3,256]{2,1,0:T(4,128)S(1)} %bitcast.101), channel_id=1, source_target_pairs={{0,4},{4,8},{8,12},{12,16},{16,20},{20,24},{24,28},{1,5},{5,9},{9,... | collective-permute-start | bytes 27656 | tf_op jit(solution)/shard_map/ppermute | solution.py:32
  215.2 1.3 collective-permute-start.8
  216.6 3.1 %collective-permute-done.8 = f32[3,3,256]{2,1,0:T(4,128)S(1)} collective-permute-done((f32[3,3,256]{2,1,0:T(4,128)S(1)}, f32[3,3,256]{2,1,0:T(4,128)S(1)}, u32[]{:S(2)}, u32[]{:S(2)}) %collective-permute-start.8) | collective-permute-done | bytes 9248 | tf_op jit(solution)/shard_map/ppermute | solution.py:32
  219.7 6.8 %collective-permute-start.10 = (f32[3,256]{1,0:T(4,128)S(1)}, f32[3,256]{1,0:T(4,128)S(1)}, u32[]{:S(2)}, u32[]{:S(2)}) collective-permute-start(f32[3,256]{1,0:T(4,128)S(1)} %bitcast.103), channel_id=1, source_target_pairs={{1,0},{2,1},{3,2},{5,4},{6,5},{7,6},{9,8},{10,9},{11,10},{13,12},{... | collective-permute-start | bytes 9224 | tf_op jit(solution)/shard_map/ppermute | solution.py:32
  226.6 3.0 %collective-permute-start.9 = (f32[3,256]{1,0:T(4,128)S(1)}, f32[3,256]{1,0:T(4,128)S(1)}, u32[]{:S(2)}, u32[]{:S(2)}) collective-permute-start(f32[3,256]{1,0:T(4,128)S(1)} %bitcast.104), channel_id=1, source_target_pairs={{0,1},{1,2},{2,3},{4,5},{5,6},{6,7},{8,9},{9,10},{10,11},{12,13},{... | collective-permute-start | bytes 9224 | tf_op jit(solution)/shard_map/ppermute | solution.py:32
  229.6 0.6 add.276
  230.4 0.6 copy.96
  (1139 shorter events, 137.6 us)
Async XLA Ops:
  14.9 13.5 %copy-start.1 = (f32[3,1,1536]{2,1,0:T(1,128)S(1)}, f32[3,1,1536]{2,1,0:T(1,128)}, u32[]{:S(2)}) copy-start(f32[3,1,1536]{2,1,0:T(1,128)} %param.19) | copy-start | bytes 55300
  14.9 13.6 %copy-start = (f32[4,1,1536]{2,1,0:T(1,128)S(1)}, f32[4,1,1536]{2,1,0:T(1,128)}, u32[]{:S(2)}) copy-start(f32[4,1,1536]{2,1,0:T(1,128)} %param.18) | copy-start | bytes 73732
  14.9 13.6 %copy-start.3 = (s32[1,1536]{1,0:T(1,128)S(1)}, s32[1,1536]{1,0:T(1,128)}, u32[]{:S(2)}) copy-start(s32[1,1536]{1,0:T(1,128)} %param.21) | copy-start | bytes 18436
  38.9 9.7 %copy-start.7 = (s32[10]{0:T(128)S(1)}, s32[10]{0:T(128)}, u32[]{:S(2)}) copy-start(s32[10]{0:T(128)} %constant.210) | copy-start | bytes 124
  38.9 9.7 %copy-start.6 = (s32[10]{0:T(128)S(1)}, s32[10]{0:T(128)}, u32[]{:S(2)}) copy-start(s32[10]{0:T(128)} %constant.211) | copy-start | bytes 124
  38.9 12.2 %copy-start.5 = (s32[16]{0:T(128)S(1)}, s32[16]{0:T(128)}, u32[]{:S(2)}) copy-start(s32[16]{0:T(128)} %constant.212) | copy-start | bytes 196
  39.1 9.7 %collective-permute-start = (f32[1,8,384]{2,0,1:T(1,128)S(1)}, f32[1,8,384]{2,0,1:T(1,128)S(1)}, u32[]{:S(2)}, u32[]{:S(2)}) collective-permute-start(f32[1,8,384]{2,0,1:T(1,128)S(1)} %bitcast.100), channel_id=1, source_target_pairs={{0,4},{4,8},{8,12},{12,16},{16,20},{20,24},{24,28},{28,0},{1,5},{5... | collective-permute-start | bytes 36872 | tf_op jit(solution)/shard_map/ppermute | solution.py:93
  41.2 10.5 %copy-start.2 = (f32[16,1,256]{2,1,0:T(1,128)S(1)}, f32[16,1,256]{2,1,0:T(1,128)}, u32[]{:S(2)}) copy-start(f32[16,1,256]{2,1,0:T(1,128)} %param.22) | copy-start | bytes 49156
  41.2 10.5 %copy-start.4 = (s32[4,1,256]{2,1,0:T(1,128)S(1)}, s32[4,1,256]{2,1,0:T(1,128)}, u32[]{:S(2)}) copy-start(s32[4,1,256]{2,1,0:T(1,128)} %param.23) | copy-start | bytes 12292
  41.3 8.6 %collective-permute-start.1 = (f32[1,8,384]{2,0,1:T(1,128)S(1)}, f32[1,8,384]{2,0,1:T(1,128)S(1)}, u32[]{:S(2)}, u32[]{:S(2)}) collective-permute-start(f32[1,8,384]{2,0,1:T(1,128)S(1)} %bitcast.99), channel_id=1, source_target_pairs={{0,8},{4,12},{8,16},{12,20},{16,24},{20,28},{24,0},{28,4},{1,9},{5... | collective-permute-start | bytes 36872 | tf_op jit(solution)/shard_map/ppermute | solution.py:93
  42.7 9.5 %collective-permute-start.2 = (f32[1,8,384]{2,0,1:T(1,128)S(1)}, f32[1,8,384]{2,0,1:T(1,128)S(1)}, u32[]{:S(2)}, u32[]{:S(2)}) collective-permute-start(f32[1,8,384]{2,0,1:T(1,128)S(1)} %bitcast.98), channel_id=1, source_target_pairs={{0,12},{4,16},{8,20},{12,24},{16,28},{20,0},{24,4},{28,8},{1,13},{... | collective-permute-start | bytes 36872 | tf_op jit(solution)/shard_map/ppermute | solution.py:93
  45.1 7.2 %collective-permute-start.3 = (f32[1,8,384]{2,0,1:T(1,128)S(1)}, f32[1,8,384]{2,0,1:T(1,128)S(1)}, u32[]{:S(2)}, u32[]{:S(2)}) collective-permute-start(f32[1,8,384]{2,0,1:T(1,128)S(1)} %bitcast.96), channel_id=1, source_target_pairs={{0,16},{4,20},{8,24},{12,28},{16,0},{20,4},{24,8},{28,12},{1,17},{... | collective-permute-start | bytes 36872 | tf_op jit(solution)/shard_map/ppermute | solution.py:93
  46.2 6.2 %collective-permute-start.4 = (f32[1,8,384]{2,0,1:T(1,128)S(1)}, f32[1,8,384]{2,0,1:T(1,128)S(1)}, u32[]{:S(2)}, u32[]{:S(2)}) collective-permute-start(f32[1,8,384]{2,0,1:T(1,128)S(1)} %bitcast.95), channel_id=1, source_target_pairs={{0,20},{4,24},{8,28},{12,0},{16,4},{20,8},{24,12},{28,16},{1,21},{... | collective-permute-start | bytes 36872 | tf_op jit(solution)/shard_map/ppermute | solution.py:93
  48.8 3.7 %collective-permute-start.5 = (f32[1,8,384]{2,0,1:T(1,128)S(1)}, f32[1,8,384]{2,0,1:T(1,128)S(1)}, u32[]{:S(2)}, u32[]{:S(2)}) collective-permute-start(f32[1,8,384]{2,0,1:T(1,128)S(1)} %bitcast.97), channel_id=1, source_target_pairs={{0,24},{4,28},{8,0},{12,4},{16,8},{20,12},{24,16},{28,20},{1,25},{... | collective-permute-start | bytes 36872 | tf_op jit(solution)/shard_map/ppermute | solution.py:93
  49.9 2.7 %collective-permute-start.6 = (f32[1,8,384]{2,0,1:T(1,128)S(1)}, f32[1,8,384]{2,0,1:T(1,128)S(1)}, u32[]{:S(2)}, u32[]{:S(2)}) collective-permute-start(f32[1,8,384]{2,0,1:T(1,128)S(1)} %bitcast.94), channel_id=1, source_target_pairs={{0,28},{4,0},{8,4},{12,8},{16,12},{20,16},{24,20},{28,24},{1,29},{... | collective-permute-start | bytes 36872 | tf_op jit(solution)/shard_map/ppermute | solution.py:93
  212.2 4.3 %collective-permute-start.7 = (f32[3,3,256]{2,1,0:T(4,128)S(1)}, f32[3,3,256]{2,1,0:T(4,128)S(1)}, u32[]{:S(2)}, u32[]{:S(2)}) collective-permute-start(f32[3,3,256]{2,1,0:T(4,128)S(1)} %bitcast.101), channel_id=1, source_target_pairs={{0,4},{4,8},{8,12},{12,16},{16,20},{20,24},{24,28},{1,5},{5,9},{9,... | collective-permute-start | bytes 27656 | tf_op jit(solution)/shard_map/ppermute | solution.py:32
  215.2 4.4 %collective-permute-start.8 = (f32[3,3,256]{2,1,0:T(4,128)S(1)}, f32[3,3,256]{2,1,0:T(4,128)S(1)}, u32[]{:S(2)}, u32[]{:S(2)}) collective-permute-start(f32[3,3,256]{2,1,0:T(4,128)S(1)} %bitcast.102), channel_id=1, source_target_pairs={{4,0},{8,4},{12,8},{16,12},{20,16},{24,20},{28,24},{5,1},{9,5},{13... | collective-permute-start | bytes 27656 | tf_op jit(solution)/shard_map/ppermute | solution.py:32
  219.7 10.5 %collective-permute-start.10 = (f32[3,256]{1,0:T(4,128)S(1)}, f32[3,256]{1,0:T(4,128)S(1)}, u32[]{:S(2)}, u32[]{:S(2)}) collective-permute-start(f32[3,256]{1,0:T(4,128)S(1)} %bitcast.103), channel_id=1, source_target_pairs={{1,0},{2,1},{3,2},{5,4},{6,5},{7,6},{9,8},{10,9},{11,10},{13,12},{... | collective-permute-start | bytes 9224 | tf_op jit(solution)/shard_map/ppermute | solution.py:32
  226.6 3.8 %collective-permute-start.9 = (f32[3,256]{1,0:T(4,128)S(1)}, f32[3,256]{1,0:T(4,128)S(1)}, u32[]{:S(2)}, u32[]{:S(2)}) collective-permute-start(f32[3,256]{1,0:T(4,128)S(1)} %bitcast.104), channel_id=1, source_target_pairs={{0,1},{1,2},{2,3},{4,5},{5,6},{6,7},{8,9},{9,10},{10,11},{12,13},{... | collective-permute-start | bytes 9224 | tf_op jit(solution)/shard_map/ppermute | solution.py:32
